TPU v7x, 256 devices: a whole 4x4x8 slice. The times are simulated.
256 devices in a mesh: grp: 8 (over z), blk: 32 (over y, x, core).
Axes of the slice: x: 4, y: 4, z: 8, core: 2. Of those that a mesh axis runs over, the one named last changes fastest.
Arguments:
- embeddings: bfloat16 [8, 2048, 1024], P('grp', 'blk'), may hold values from -72 to 72
- cluster_ids: int32 [8, 2048], P('grp', 'blk'), may hold values from 0 to 63, never falling along the last dimension, each value on 1 to 128 neighbouring positions
- block_list: int32 [8, 256, 2], P('grp', 'blk'), may hold values from 0 to 31, as said below
- block_counts: int32 [8, 32], P('grp', 'blk'), may hold values from 1 to 8, as said below
- pair_targets: float32 [8, 256, 4096], P('grp', 'blk'), may hold values from -6 to 6
- w_left: bfloat16 [1024, 512], replicated, may hold values from -0.125 to 0.125
- w_right: bfloat16 [1024, 512], replicated, may hold values from -0.125 to 0.125
- hidden_bias: float32 [512], replicated, may hold values from -3 to 3
- w_middle: bfloat16 [512, 128], replicated, may hold values from -0.25 to 0.25
- w_final: float32 [128], replicated, may hold values from -0.5 to 0.5
Outputs:
- grad_embeddings: float32 [8, 2048, 1024], P('grp', 'blk')
- grad_left: float32 [1024, 512], replicated
- grad_right: float32 [1024, 512], replicated
- grad_bias: float32 [512], replicated
- grad_middle: float32 [512, 128], replicated
- grad_final: float32 [128], replicated
Inputs may be any that keep to these rules, and one draw needn't show every extreme that they name: `block_list`: entries are panels of the device's own group; the column panel lies within one of the row panel. `block_counts`: slots of a device at and beyond its count are unused; in every group one device has exactly 8.
All inputs are finite; a program needn't handle non-finite values.
Results may differ from a plain program's by a relative error of at most 0.012.
Values may be sent and summed in bfloat16 or wider, within the bound.
No kernel may reach another device: no remote copies, remote signals or barrier semaphores. Data moves between devices by JAX's collectives and lax.ppermute only.
A program may use at most 128 MiB of HBM per device.

v0:
```python
import math
import jax
import jax.numpy as jnp
from jax import lax
from jax.sharding import PartitionSpec as P

PANEL = 64
B_DEV = 8


def silu_slope(value):
    sigmoid_value = jax.nn.sigmoid(value)
    return sigmoid_value * (1.0 + value * (1.0 - sigmoid_value))


def pair_block(
    left_rows,
    right_rows,
    left_ids,
    right_ids,
    row_start,
    col_start,
    pair_target,
    hidden_bias,
    w_middle,
    w_final,
):
    panel_rows = left_rows.shape[0]
    hidden_width = left_rows.shape[1]
    pre_hidden = (
        left_rows.astype(jnp.float32)[:, None, :]
        + right_rows.astype(jnp.float32)[None, :, :]
        + hidden_bias
    )
    hidden = (
        jax.nn.silu(pre_hidden).astype(jnp.bfloat16).reshape(panel_rows * panel_rows, hidden_width)
    )
    pre_upper = jnp.dot(hidden, w_middle, preferred_element_type=jnp.float32)
    upper_act = jax.nn.silu(pre_upper)
    predicted = jnp.sum(upper_act * w_final, axis=1)
    left_pos = row_start + jnp.arange(panel_rows, dtype=jnp.int32)
    right_pos = col_start + jnp.arange(panel_rows, dtype=jnp.int32)
    same_cluster = (left_ids[:, None] == right_ids[None, :]) & (
        left_pos[:, None] != right_pos[None, :]
    )
    residual = jnp.where(same_cluster.reshape(-1), predicted - pair_target, 0.0)
    pair_slope = 16.0 * residual
    grad_final = jnp.sum(upper_act * pair_slope[:, None], axis=0)
    grad_second = (pair_slope[:, None] * w_final[None, :] * silu_slope(pre_upper)).astype(
        jnp.bfloat16
    )
    grad_middle = lax.dot_general(
        hidden, grad_second, (((0,), (0,)), ((), ())), preferred_element_type=jnp.float32
    )
    grad_hidden = lax.dot_general(
        grad_second, w_middle, (((1,), (1,)), ((), ())), preferred_element_type=jnp.float32
    )
    grad_first = grad_hidden.reshape(panel_rows, panel_rows, hidden_width) * silu_slope(pre_hidden)
    return (
        jnp.sum(grad_first, axis=1),
        jnp.sum(grad_first, axis=0),
        jnp.sum(grad_first, axis=(0, 1)),
        grad_middle,
        grad_final,
    )


def local(
    embeddings,
    cluster_ids,
    block_list,
    block_counts,
    pair_targets,
    w_left,
    w_right,
    hidden_bias,
    w_middle,
    w_final,
):
    local_emb = embeddings[0]
    whole_emb, group_ids = (
        lax.all_gather(embeddings, "blk", axis=1, tiled=True),
        lax.all_gather(cluster_ids, "blk", axis=1, tiled=True),
    )
    whole_emb = whole_emb[0]

    def fetch_panels(row_start, col_start):
        row_emb = lax.dynamic_slice_in_dim(whole_emb, row_start, PANEL, 0)
        col_emb = lax.dynamic_slice_in_dim(whole_emb, col_start, PANEL, 0)
        return (
            jnp.dot(row_emb, w_left, preferred_element_type=jnp.float32).astype(jnp.bfloat16),
            jnp.dot(col_emb, w_right, preferred_element_type=jnp.float32).astype(jnp.bfloat16),
        )

    group_ids = group_ids[0]
    local_blocks = block_list[0]
    local_targets = pair_targets[0]
    molecules = group_ids.shape[0]
    hidden_width = w_left.shape[1]

    def slot_step(slot, carry):
        part_left, part_right, sum_bias, sum_middle, sum_final = carry
        entry = lax.dynamic_index_in_dim(local_blocks, slot, 0, keepdims=False)
        row_start = entry[0] * PANEL
        col_start = entry[1] * PANEL
        pair_target = lax.dynamic_index_in_dim(local_targets, slot, 0, keepdims=False)
        left_rows, right_rows = fetch_panels(row_start, col_start)
        grad_rows, grad_cols, grad_bias, grad_middle, grad_final = pair_block(
            left_rows,
            right_rows,
            lax.dynamic_slice_in_dim(group_ids, row_start, PANEL, 0),
            lax.dynamic_slice_in_dim(group_ids, col_start, PANEL, 0),
            row_start,
            col_start,
            pair_target,
            hidden_bias,
            w_middle,
            w_final,
        )
        current = lax.dynamic_slice_in_dim(part_left, row_start, PANEL, 0)
        part_left = lax.dynamic_update_slice_in_dim(part_left, current + grad_rows, row_start, 0)
        current = lax.dynamic_slice_in_dim(part_right, col_start, PANEL, 0)
        part_right = lax.dynamic_update_slice_in_dim(part_right, current + grad_cols, col_start, 0)
        return (
            part_left,
            part_right,
            sum_bias + grad_bias,
            sum_middle + grad_middle,
            sum_final + grad_final,
        )

    empty = jnp.zeros((molecules, hidden_width), jnp.float32)
    start_state = (
        empty,
        empty,
        jnp.zeros((hidden_width,), jnp.float32),
        jnp.zeros(w_middle.shape, jnp.float32),
        jnp.zeros(w_final.shape, jnp.float32),
    )
    part_left, part_right, sum_bias, sum_middle, sum_final = lax.fori_loop(
        0, block_counts[0, 0], slot_step, start_state
    )
    rounded_left = part_left.astype(jnp.bfloat16)
    rounded_right = part_right.astype(jnp.bfloat16)
    own_left, own_right = (
        lax.psum_scatter(
            rounded_left.astype(jnp.float32).astype(jnp.bfloat16),
            "blk",
            scatter_dimension=0,
            tiled=True,
        ).astype(jnp.float32),
        lax.psum_scatter(
            rounded_right.astype(jnp.float32).astype(jnp.bfloat16),
            "blk",
            scatter_dimension=0,
            tiled=True,
        ).astype(jnp.float32),
    )
    left_grad = own_left.astype(jnp.bfloat16)
    right_grad = own_right.astype(jnp.bfloat16)
    grad_local = jnp.dot(left_grad, w_left.T, preferred_element_type=jnp.float32) + jnp.dot(
        right_grad, w_right.T, preferred_element_type=jnp.float32
    )
    weight_left = lax.dot_general(
        local_emb, left_grad, (((0,), (0,)), ((), ())), preferred_element_type=jnp.float32
    )
    weight_right = lax.dot_general(
        local_emb, right_grad, (((0,), (0,)), ((), ())), preferred_element_type=jnp.float32
    )
    summed = lax.psum((weight_left, weight_right, sum_bias, sum_middle, sum_final), ("grp", "blk"))
    devices = lax.axis_size("grp") * lax.axis_size("blk")
    scale = 1.0 / math.sqrt(devices * B_DEV * PANEL)
    return (
        grad_local[None],
        summed[0] * scale,
        summed[1] * scale,
        summed[2] * scale,
        summed[3] * scale,
        summed[4] * scale,
    )


def solution(mesh):
    return jax.shard_map(
        local,
        mesh=mesh,
        in_specs=(
            P("grp", "blk", None),
            P("grp", "blk"),
            P("grp", "blk", None),
            P("grp", "blk"),
            P("grp", "blk", None),
            P(),
            P(),
            P(),
            P(),
            P(),
        ),
        out_specs=(P("grp", "blk", None), P(), P(), P(), P(), P()),
        check_vma=False,
    )
```

profile of v0, /device:TPU:2, one launch (start us, length us, event | category | flops | bytes accessed | tf_op | source)
XLA Modules:
  0.0 784.3 jit_solution(16809696372307641489)
XLA Ops:
  10.7 15.9 %all-reduce = s32[2048]{0:T(1024)S(1)} all-reduce(s32[2048]{0:T(1024)S(1)} %bitcast_dynamic-update-slice_fusion), channel_id=1, replica_groups=mesh['grp'=8,'blk'=32] {'blk'}, use_global_device_ids=true, to_apply=%add | all-reduce | flops 2048 | bytes 16384 | tf_op jit(solution)/shard_map/squeeze | solution.py:95
  26.5 37.7 %all-gather.2.cloned.1.call-done = bf16[1,2048,1024]{2,1,0:T(8,128)(2,1)} async-done(((bf16[1,64,1024]{2,1,0:T(8,128)(2,1)}), bf16[1,2048,1024]{2,1,0:T(8,128)(2,1)}) %all-gather.2.cloned.1.call-update) | async-done | bytes 4194320 | tf_op jit(solution)/shard_map/all_gather | solution.py:82
  64.3 2.5 broadcast_in_dim.14
  66.7 2.5 broadcast_in_dim.14.clone
  70.0 60.5 %while.18 = (s32[]{:T(128)}, f32[2048,512]{1,0:T(8,128)}, f32[2048,512]{1,0:T(8,128)}, f32[512]{0:T(512)S(1)}, f32[512,128]{1,0:T(8,128)}, /*index=5*/f32[128]{0...) while((s32[]{:T(128)}, f32[2048,512]{1,0:T(8,128)}, ...), condition=%wide.region_6.7_spmd, body=%wide.region_0.6_spmd.sunk | while | flops 1822642304 | bytes 153014800 | solution.py:140
  76.5 3.4 multiply_convert_fusion.7
  83.1 5.0 convolution_add_fusion.3
  88.1 5.3 multiply_reduce_fusion.7
  93.4 3.9 fusion.52
  106.3 3.4 multiply_convert_fusion.7
  112.9 5.0 convolution_add_fusion.3
  118.0 5.3 multiply_reduce_fusion.7
  123.2 3.9 fusion.52
  130.5 3.8 convert_element_type.34
  134.3 3.8 convert_element_type.33
  138.2 261.0 %reduce-scatter.5.cloned.1.call-done = bf16[64,512]{1,0:T(8,128)(2,1)} async-done(((bf16[2048,512]{1,0:T(8,128)(2,1)}), bf16[64,512]{1,0:T(8,128)(2,1)}) %reduce-scatter.5.cloned.1.call-update) | async-done | bytes 65552 | tf_op jit(solution)/shard_map/reduce_scatter | solution.py:152
  399.2 2.6 convolution_bitcast_fusion
  401.8 87.8 %reduce-scatter.3.cloned.1.call-done = bf16[64,512]{1,0:T(8,128)(2,1)} async-done(((bf16[2048,512]{1,0:T(8,128)(2,1)}), bf16[64,512]{1,0:T(8,128)(2,1)}) %reduce-scatter.3.cloned.1.call-update) | async-done | bytes 65552 | tf_op jit(solution)/shard_map/reduce_scatter | solution.py:146
  489.6 2.7 convolution_bitcast_fusion.1
  492.3 73.9 %all-reduce.1 = (f32[512]{0:T(512)S(1)}, f32[128]{0:T(128)S(1)}) all-reduce(f32[512]{0:T(512)S(1)} %get-tuple-element.95, f32[128]{0:T(128)S(1)} %get-tuple-element.97), channel_id=1, replica_groups=mesh['grp'=8,'blk'=32] {'grp','blk'}, use_global_device_ids=true, to_apply=%region_11.12 | all-reduce | flops 640 | bytes 5120 | tf_op jit(solution)/shard_map/psum | solution.py:170
  567.7 2.4 fusion.8
  570.1 198.0 %all-reduce.5.cloned.1.call-done = (f32[1024,512]{0,1:T(8,128)}, f32[1024,512]{0,1:T(8,128)}, f32[512,128]{1,0:T(8,128)}) async-done(((f32[1024,512]{0,1:T(8,128)}, f32[1024,512]{0,1:T(8,128)}, f32[512,128]{1,0:T(8,128)}), (f32[1024,512]{0,1:T(8,128)}, f32[1024,512]{0,1:T(8,128)}, f32[512,128]{1,0:T(8,128)})) %all-reduce.5.cloned.1.call-update) | async-done | bytes 4456464 | tf_op jit(solution)/shard_map/psum | solution.py:170
  768.1 4.2 broadcast_multiply_fusion
  772.3 2.9 copy.16
  (89 shorter events, 27.9 us)
Async XLA Ops:
  7.2 57.1 %all-gather.2.cloned.1.call-start = ((), (), s32[]{:S(2)}) async-start(), calls=%async_computation.2 | async-start | bytes 4325376 | tf_op jit(solution)/shard_map/all_gather | solution.py:82
  7.9 391.3 %reduce-scatter.5.cloned.1.call-start = ((), (), s32[]{:S(2)}) async-start(), calls=%async_computation.4 | async-start | bytes 2162688 | tf_op jit(solution)/shard_map/reduce_scatter | solution.py:152
  64.2 5.7 copy-start.3
  64.3 5.7 copy-start.8
  64.3 5.7 copy-start.9
  64.3 5.7 copy-start.12
  76.5 3.4 copy-start
  76.5 3.4 copy-start.10
  79.9 2.0 copy-start.2
  83.1 5.1 copy-start.1
  83.1 5.1 copy-start.11
  106.3 3.4 copy-start
  106.3 3.4 copy-start.10
  109.7 2.0 copy-start.2
  112.9 5.1 copy-start.1
  112.9 5.1 copy-start.11
  134.3 355.3 %reduce-scatter.3.cloned.1.call-start = ((), (), s32[]{:S(2)}) async-start(), calls=%async_computation.3 | async-start | bytes 2162688 | tf_op jit(solution)/shard_map/reduce_scatter | solution.py:146
  134.3 264.9 %copy-start.4 = (bf16[1,64,1024]{2,1,0:T(8,128)(2,1)S(1)}, bf16[1,64,1024]{2,1,0:T(8,128)(2,1)}, u32[]{:S(2)}) copy-start(bf16[1,64,1024]{2,1,0:T(8,128)(2,1)} %param.12) | copy-start | bytes 393220
  138.2 629.9 %all-reduce.5.cloned.1.call-start = ((), (), s32[]{:S(2)}) async-start(), calls=%async_computation.5 | async-start | bytes 8912896 | tf_op jit(solution)/shard_map/psum | solution.py:170
  401.8 165.9 %copy-start.5 = (bf16[64,512]{1,0:T(8,128)(2,1)S(1)}, bf16[64,512]{1,0:T(8,128)(2,1)}, u32[]{:S(2)}) copy-start(bf16[64,512]{1,0:T(8,128)(2,1)} %reduce-scatter.5.cloned.1.call-done) | copy-start | bytes 196612
  489.6 77.7 %copy-start.7 = (bf16[64,512]{1,0:T(8,128)(2,1)S(1)}, bf16[64,512]{1,0:T(8,128)(2,1)}, u32[]{:S(2)}) copy-start(bf16[64,512]{1,0:T(8,128)(2,1)} %reduce-scatter.3.cloned.1.call-done) | copy-start | bytes 196612
  772.3 4.7 copy-start.6
Sparse Core Ops, SparseCore 0:
  10.5 53.6 all-gather.1
  134.4 264.7 reduce-scatter.4
  403.6 85.9 reduce-scatter.2
  495.8 272.2 all-reduce.4
where the time goes:
time: 786 us; the launch traced here: 784 us
  waiting for transfers between devices  585 us (74%)
  blocking collectives  89.8 us (11%)
  matrix products  37 us (5%)
  other arithmetic  35.6 us (5%)
  local copies, waits for them, and re-layouts  17.1 us (2%)
  between operations  14.5 us (2%)
    reduce_scatter x1, waiting for transfers between devices, local(): lax.psum_scatter(rounded_right.astype(jnp.float32).astype(jnp.bfloat16),...  261 us
    psum x1, waiting for transfers between devices, local(): lax.psum((weight_left, weight_right, sum_bias, sum_middle, sum_final), ('...  198 us
    reduce_scatter x1, waiting for transfers between devices, local(): lax.psum_scatter(rounded_left.astype(jnp.float32).astype(jnp.bfloat16), '...  87.8 us
    psum x1, blocking collectives, local(): lax.psum((weight_left, weight_right, sum_bias, sum_middle, sum_final), ('...  73.9 us
    all_gather x1, waiting for transfers between devices, local(): lax.all_gather(embeddings, 'blk', axis=1, tiled=True)  37.7 us
    squeeze x1, blocking collectives, local(): group_ids = group_ids[0]  15.9 us
  transfers between devices with their start and end apart: 4, of which 4 were waited for; matrix products, arithmetic and copies ran while one was open for 2% of the time, Pallas kernels for 0%

commit v1 on v0

--- a/solution.py
+++ b/solution.py
@@ -167,7 +167,9 @@
     weight_right = lax.dot_general(
         local_emb, right_grad, (((0,), (0,)), ((), ())), preferred_element_type=jnp.float32
     )
-    summed = lax.psum((weight_left, weight_right, sum_bias, sum_middle, sum_final), ("grp", "blk"))
+    summed = lax.psum(
+        lax.psum((weight_left, weight_right, sum_bias, sum_middle, sum_final), "blk"), "grp"
+    )
     devices = lax.axis_size("grp") * lax.axis_size("blk")
     scale = 1.0 / math.sqrt(devices * B_DEV * PANEL)
     return (

time: 786 us -> 751 us (0.955)
  waiting for transfers between devices: 585 us -> 544 us
    psum x1 -> x2, waiting for transfers between devices: 198 us -> 157 us  [the longest x1 123 us: local(): lax.psum((weight_left, weight_right, sum_bias, sum_middle, sum_final), 'b...]
    psum x1 -> x2, blocking collectives: 73.9 us -> 79.6 us  [the longest x1 61.8 us: local(): lax.psum((weight_left, weight_right, sum_bias, sum_middle, sum_final), 'b...]
  transfers between devices with their start and end apart: 4 -> 5, of which waited for: 4 -> 5; matrix products, arithmetic and copies ran while one was open for 2% -> 2% of each run, Pallas kernels for 0% -> 0%
where the time goes in v1:
time: 751 us; the launch traced here: 749 us
  waiting for transfers between devices  544 us (72%)
  blocking collectives  95.5 us (13%)
  matrix products  36.9 us (5%)
  other arithmetic  35.6 us (5%)
  local copies, waits for them, and re-layouts  17.1 us (2%)
  between operations  14.5 us (2%)
    reduce_scatter x1, waiting for transfers between devices, local(): lax.psum_scatter(rounded_right.astype(jnp.float32).astype(jnp.bfloat16),...  261 us
    psum x1, waiting for transfers between devices, local(): lax.psum((weight_left, weight_right, sum_bias, sum_middle, sum_final), 'b...  123 us
    reduce_scatter x1, waiting for transfers between devices, local(): lax.psum_scatter(rounded_left.astype(jnp.float32).astype(jnp.bfloat16), '...  87.8 us
    psum x1, blocking collectives, local(): lax.psum((weight_left, weight_right, sum_bias, sum_middle, sum_final), 'b...  61.8 us
    all_gather x1, waiting for transfers between devices, local(): lax.all_gather(embeddings, 'blk', axis=1, tiled=True)  37.7 us
    psum x1, waiting for transfers between devices, local(): lax.psum(lax.psum((weight_left, weight_right, sum_bias, sum_middle, sum_f...  33.4 us
    psum x1, blocking collectives, local(): lax.psum(lax.psum((weight_left, weight_right, sum_bias, sum_middle, sum_f...  17.9 us
    squeeze x1, blocking collectives, local(): group_ids = group_ids[0]  15.9 us
  transfers between devices with their start and end apart: 5, of which 5 were waited for; matrix products, arithmetic and copies ran while one was open for 2% of the time, Pallas kernels for 0%

profile of v1, /device:TPU:2, one launch (start us, length us, event | category | flops | bytes accessed | tf_op | source)
XLA Modules:
  0.0 748.6 jit_solution(13064960240380945875)
XLA Ops:
  10.7 15.9 %all-reduce = s32[2048]{0:T(1024)S(1)} all-reduce(s32[2048]{0:T(1024)S(1)} %bitcast_dynamic-update-slice_fusion), channel_id=1, replica_groups=mesh['grp'=8,'blk'=32] {'blk'}, use_global_device_ids=true, to_apply=%add | all-reduce | flops 2048 | bytes 16384 | tf_op jit(solution)/shard_map/squeeze | solution.py:95
  26.5 37.7 %all-gather.2.cloned.1.call-done = bf16[1,2048,1024]{2,1,0:T(8,128)(2,1)} async-done(((bf16[1,64,1024]{2,1,0:T(8,128)(2,1)}), bf16[1,2048,1024]{2,1,0:T(8,128)(2,1)}) %all-gather.2.cloned.1.call-update) | async-done | bytes 4194320 | tf_op jit(solution)/shard_map/all_gather | solution.py:82
  64.3 2.5 broadcast_in_dim.14
  70.0 60.5 %while.18 = (s32[]{:T(128)}, f32[2048,512]{1,0:T(8,128)}, f32[2048,512]{1,0:T(8,128)}, f32[512]{0:T(512)S(1)}, f32[512,128]{1,0:T(8,128)}, /*index=5*/f32[128]{0...) while((s32[]{:T(128)}, f32[2048,512]{1,0:T(8,128)}, ...), condition=%wide.region_6.7_spmd, body=%wide.region_0.6_spmd.sunk | while | flops 1822642304 | bytes 153014800 | solution.py:140
  76.5 3.4 multiply_convert_fusion.7
  83.1 5.0 convolution_add_fusion.3
  88.1 5.3 multiply_reduce_fusion.7
  93.4 3.9 fusion.52
  106.3 3.4 multiply_convert_fusion.7
  112.9 5.0 convolution_add_fusion.3
  118.0 5.3 multiply_reduce_fusion.7
  123.2 3.9 fusion.52
  130.5 3.8 convert_element_type.34
  134.3 3.8 convert_element_type.33
  138.2 261.0 %reduce-scatter.5.cloned.1.call-done = bf16[64,512]{1,0:T(8,128)(2,1)} async-done(((bf16[2048,512]{1,0:T(8,128)(2,1)}), bf16[64,512]{1,0:T(8,128)(2,1)}) %reduce-scatter.5.cloned.1.call-update) | async-done | bytes 65552 | tf_op jit(solution)/shard_map/reduce_scatter | solution.py:152
  399.2 2.6 convolution_bitcast_fusion
  401.8 87.8 %reduce-scatter.3.cloned.1.call-done = bf16[64,512]{1,0:T(8,128)(2,1)} async-done(((bf16[2048,512]{1,0:T(8,128)(2,1)}), bf16[64,512]{1,0:T(8,128)(2,1)}) %reduce-scatter.3.cloned.1.call-update) | async-done | bytes 65552 | tf_op jit(solution)/shard_map/reduce_scatter | solution.py:146
  489.6 2.6 convolution_bitcast_fusion.1
  492.3 123.1 %all-reduce.8.cloned.1.call-done = (f32[1024,512]{0,1:T(8,128)}, f32[1024,512]{0,1:T(8,128)}, f32[512,128]{1,0:T(8,128)}) async-done(((f32[1024,512]{0,1:T(8,128)}, f32[1024,512]{0,1:T(8,128)}, f32[512,128]{1,0:T(8,128)}), (f32[1024,512]{0,1:T(8,128)}, f32[1024,512]{0,1:T(8,128)}, f32[512,128]{1,0:T(8,128)})) %all-reduce.8.cloned.1.call-update) | async-done | bytes 4456464 | tf_op jit(solution)/shard_map/psum | solution.py:171
  615.4 61.8 %all-reduce.1 = (f32[512]{0:T(512)S(1)}, f32[128]{0:T(128)S(1)}) all-reduce(f32[512]{0:T(512)S(1)} %get-tuple-element.95, f32[128]{0:T(128)S(1)} %get-tuple-element.97), channel_id=1, replica_groups=mesh['grp'=8,'blk'=32] {'blk'}, use_global_device_ids=true, to_apply=%region_13.14 | all-reduce | flops 640 | bytes 5120 | tf_op jit(solution)/shard_map/psum | solution.py:171
  677.2 17.9 %all-reduce.3 = (f32[512]{0:T(512)S(1)}, f32[128]{0:T(128)S(1)}) all-reduce(f32[512]{0:T(512)S(1)} %get-tuple-element.138, f32[128]{0:T(128)S(1)} %get-tuple-element.139), channel_id=1, replica_groups=mesh['grp'=8,'blk'=32] {'grp'}, use_global_device_ids=true, to_apply=%region_14.15 | all-reduce | flops 640 | bytes 5120 | tf_op jit(solution)/shard_map/psum | solution.py:170
  698.9 33.4 %all-reduce.10.cloned.1.call-done = (f32[1024,512]{0,1:T(8,128)}, f32[1024,512]{0,1:T(8,128)}, f32[512,128]{1,0:T(8,128)}) async-done(((f32[1024,512]{0,1:T(8,128)}, f32[1024,512]{0,1:T(8,128)}, f32[512,128]{1,0:T(8,128)}), (f32[1024,512]{0,1:T(8,128)}, f32[1024,512]{0,1:T(8,128)}, f32[512,128]{1,0:T(8,128)})) %all-reduce.10.cloned.1.call-update) | async-done | bytes 4456464 | tf_op jit(solution)/shard_map/psum | solution.py:170
  732.3 4.2 broadcast_multiply_fusion
  736.6 2.9 copy.16
  (93 shorter events, 32.8 us)
Async XLA Ops:
  7.2 57.1 %all-gather.2.cloned.1.call-start = ((), (), s32[]{:S(2)}) async-start(), calls=%async_computation.2 | async-start | bytes 4325376 | tf_op jit(solution)/shard_map/all_gather | solution.py:82
  7.9 391.3 %reduce-scatter.5.cloned.1.call-start = ((), (), s32[]{:S(2)}) async-start(), calls=%async_computation.4 | async-start | bytes 2162688 | tf_op jit(solution)/shard_map/reduce_scatter | solution.py:152
  64.2 5.7 copy-start.3
  64.3 5.7 copy-start.8
  64.3 5.7 copy-start.9
  64.3 5.7 copy-start.12
  76.5 3.4 copy-start
  76.5 3.4 copy-start.10
  79.9 2.0 copy-start.2
  83.1 5.1 copy-start.1
  83.1 5.1 copy-start.11
  106.3 3.4 copy-start
  106.3 3.4 copy-start.10
  109.7 2.0 copy-start.2
  112.9 5.1 copy-start.1
  112.9 5.1 copy-start.11
  134.3 355.3 %reduce-scatter.3.cloned.1.call-start = ((), (), s32[]{:S(2)}) async-start(), calls=%async_computation.3 | async-start | bytes 2162688 | tf_op jit(solution)/shard_map/reduce_scatter | solution.py:146
  134.3 264.9 %copy-start.4 = (bf16[1,64,1024]{2,1,0:T(8,128)(2,1)S(1)}, bf16[1,64,1024]{2,1,0:T(8,128)(2,1)}, u32[]{:S(2)}) copy-start(bf16[1,64,1024]{2,1,0:T(8,128)(2,1)} %param.12) | copy-start | bytes 393220
  138.2 477.2 %all-reduce.8.cloned.1.call-start = ((), (), s32[]{:S(2)}) async-start(), calls=%async_computation.5 | async-start | bytes 8912896 | tf_op jit(solution)/shard_map/psum | solution.py:171
  492.2 203.9 %copy-start.7 = (bf16[64,512]{1,0:T(8,128)(2,1)S(1)}, bf16[64,512]{1,0:T(8,128)(2,1)}, u32[]{:S(2)}) copy-start(bf16[64,512]{1,0:T(8,128)(2,1)} %reduce-scatter.3.cloned.1.call-done) | copy-start | bytes 196612
  492.2 204.4 %copy-start.5 = (bf16[64,512]{1,0:T(8,128)(2,1)S(1)}, bf16[64,512]{1,0:T(8,128)(2,1)}, u32[]{:S(2)}) copy-start(bf16[64,512]{1,0:T(8,128)(2,1)} %reduce-scatter.5.cloned.1.call-done) | copy-start | bytes 196612
  492.2 240.1 %all-reduce.10.cloned.1.call-start = ((), (), s32[]{:S(2)}) async-start(), calls=%async_computation.6 | async-start | bytes 8912896 | tf_op jit(solution)/shard_map/psum | solution.py:170
  736.6 4.7 copy-start.6
Sparse Core Ops, SparseCore 0:
  10.5 53.6 all-gather.1
  134.4 264.7 reduce-scatter.4
  403.6 85.9 reduce-scatter.2
  493.7 121.6 all-reduce.7
  617.8 114.4 all-reduce.9
